TPU v7x, 32 devices: a whole 2x2x4 slice. The times are simulated.
32 devices in a mesh: dp: 16 (over z, y, core), mp: 2 (over x).
Axes of the slice: x: 2, y: 2, z: 4, core: 2. Of those that a mesh axis runs over, the one named last changes fastest.
Arguments:
- tokens: bfloat16 [32768, 768], P('dp'), may hold values from -6 to 6
- grad_out: bfloat16 [32768, 768], P('dp'), may hold values from -6 to 6
- head_perm: int32 [32, 12], P('dp', 'mp'), may hold values from 0 to 1
- block_mask: int32 [32, 12, 3], P('dp', 'mp'), may hold values 0 or 1
- w_qkv: bfloat16 [768, 3, 768], P('dp', None, 'mp'), may hold values from -0.3125 to 0.3125
- b_qv: bfloat16 [2, 768], P(None, ('mp', 'dp')), may hold values from -3 to 3
- w_out: bfloat16 [768, 768], P('mp', 'dp'), may hold values from -0.625 to 0.625
- b_out: bfloat16 [768], P('dp'), may hold values from -3 to 3
- gain_one: bfloat16 [768], P('dp'), may hold values from 0.25 to 1.75
- shift_one: bfloat16 [768], P('dp'), may hold values from -2 to 2
- w_up: bfloat16 [768, 3072], P('dp', 'mp'), may hold values from -0.21875 to 0.21875
- b_up: bfloat16 [3072], P(('mp', 'dp')), may hold values from -3 to 3
- w_down: bfloat16 [3072, 768], P('mp', 'dp'), may hold values from -0.15625 to 0.15625
- b_down: bfloat16 [768], P('dp'), may hold values from -2 to 2
- gain_two: bfloat16 [768], P('dp'), may hold values from 0.25 to 1.75
- shift_two: bfloat16 [768], P('dp'), may hold values from -2 to 2
Outputs:
- output: bfloat16 [32768, 768], P('dp')
- input_grad: float32 [32768, 768], P('dp')
- grad_w_qkv: float32 [768, 3, 768], P('dp', None, 'mp')
- grad_b_qv: float32 [2, 768], P(None, ('mp', 'dp'))
- grad_w_out: float32 [768, 768], P('mp', 'dp')
- grad_b_out: float32 [768], P('dp')
- grad_gain_one: float32 [768], P('dp')
- grad_shift_one: float32 [768], P('dp')
- grad_w_up: float32 [768, 3072], P('dp', 'mp')
- grad_b_up: float32 [3072], P(('mp', 'dp'))
- grad_w_down: float32 [3072, 768], P('mp', 'dp')
- grad_b_down: float32 [768], P('dp')
- grad_gain_two: float32 [768], P('dp')
- grad_shift_two: float32 [768], P('dp')
Inputs may be any that keep to these rules, and one draw needn't show every extreme that they name: `head_perm`: 0 pairs each half with itself, 1 pairs it with the other half. `block_mask`: entry a + b is the keep flag of block a of the queries with block b of the keys (b <= a).
All inputs are finite; a program needn't handle non-finite values.
Results may differ from a plain program's by a relative error of at most 0.015.
The roundings to bfloat16 on the way count: a program that leaves them out, or rounds other values in their place, can miss the bound.
Values may be sent and summed in bfloat16 or wider, within the bound.
No kernel may reach another device: no remote copies, remote signals or barrier semaphores. Data moves between devices by JAX's collectives and lax.ppermute only.
A program may use at most 256 MiB of HBM per device.

v0:
```python
import jax
import jax.numpy as jnp
from jax import lax
from jax.sharding import PartitionSpec as P

HD = 64
norm_eps = 1e-05
masked_fill = -1e30


def layer_norm(hidden, gain_vec, shift_vec):
    centered = hidden - jnp.mean(hidden, axis=-1, keepdims=True)
    variance = jnp.mean(centered * centered, axis=-1, keepdims=True)
    return centered * lax.rsqrt(variance + norm_eps) * gain_vec + shift_vec


def gelu_exact(values):
    return jax.nn.gelu(values, approximate=False)


def contract_rows(first_mat, second_mat):
    return lax.dot_general(
        first_mat, second_mat, (((0,), (0,)), ((), ())), preferred_element_type=jnp.float32
    )


def contract_cols(first_mat, second_mat):
    return lax.dot_general(
        first_mat, second_mat, (((1,), (1,)), ((), ())), preferred_element_type=jnp.float32
    )


def pair_pattern(mask_rows, half_len, block_len):
    blocks = jnp.arange(half_len) // block_len
    row_block = blocks[:, None]
    col_block = blocks[None, :]
    entry_index = row_block + col_block
    chosen = jnp.zeros((mask_rows.shape[0], half_len, half_len), dtype=jnp.bool_)
    for entry_id in range(3):
        chosen = (
            chosen | (mask_rows[:, entry_id, None, None] == 1) & (entry_index == entry_id)[None]
        )
    allowed = chosen & (col_block <= row_block)[None]
    allowed_f = allowed.astype(jnp.float32)
    dead_f = 1.0 - jnp.max(allowed_f, axis=-1)
    return (allowed, allowed_f, dead_f)


def pair_keys(values, swapped):
    return jnp.where(swapped[None, :, None], jnp.roll(values, values.shape[0] // 2, axis=0), values)


def split_pairs(proj_low, perm_seq, head_count):
    seq_len = proj_low.shape[0]
    half_len = seq_len // 2
    split_heads = proj_low.reshape(seq_len, 3, head_count, HD)
    swapped = perm_seq == 1
    query_pair = split_heads[:, 0].reshape(2, half_len, head_count, HD)
    key_pair = pair_keys(split_heads[:, 1], swapped).reshape(2, half_len, head_count, HD)
    value_pair = pair_keys(split_heads[:, 2], swapped).reshape(2, half_len, head_count, HD)
    return (query_pair, key_pair, value_pair, swapped)


def masked_scores(query_pair, key_pair, allowed):
    raw_scores = jnp.einsum(
        "iqhd,ikhd->ihqk", query_pair, key_pair, preferred_element_type=jnp.float32
    ) * HD ** (-0.5)
    return jnp.where(allowed[None], raw_scores, masked_fill)


def forward_pass(tokens_seq, perm_seq, mask_seq, weights):
    (
        w_qkv,
        b_qv,
        w_out,
        b_out,
        gain_one,
        shift_one,
        w_up,
        b_up,
        w_down,
        b_down,
        gain_two,
        shift_two,
    ) = weights
    seq_len = tokens_seq.shape[0]
    half_len = seq_len // 2
    local_width = w_qkv.shape[2]
    head_count = local_width // HD
    projected = jnp.einsum("td,dcf->tcf", tokens_seq, w_qkv, preferred_element_type=jnp.float32)
    bias_rows = jnp.stack([b_qv[0], jnp.zeros_like(b_qv[0]), b_qv[1]]).astype(jnp.float32)
    proj_low = (projected + bias_rows[None]).astype(jnp.bfloat16)
    query_pair, key_pair, value_pair, swapped = split_pairs(proj_low, perm_seq, head_count)
    allowed, allowed_f, dead_f = pair_pattern(mask_seq, half_len, half_len // 2)
    masked = masked_scores(query_pair, key_pair, allowed)
    row_max = jnp.max(masked, axis=-1)
    row_total = jnp.sum(jnp.exp(masked - row_max[..., None]) * allowed_f[None], axis=-1)
    log_total = row_max + jnp.log(row_total + dead_f[None])
    attn_weights = (jnp.exp(masked - log_total[..., None]) * allowed_f[None]).astype(jnp.bfloat16)
    context = jnp.einsum(
        "ihqk,ikhd->iqhd", attn_weights, value_pair, preferred_element_type=jnp.float32
    )
    context_low = context.reshape(seq_len, local_width).astype(jnp.bfloat16)
    attn_part = jnp.dot(context_low, w_out, preferred_element_type=jnp.float32)
    attn_out = lax.psum(attn_part, "mp")
    resid_one = tokens_seq.astype(jnp.float32) + attn_out + b_out.astype(jnp.float32)
    normed_one = layer_norm(resid_one, gain_one.astype(jnp.float32), shift_one.astype(jnp.float32))
    normed_share = normed_one.astype(jnp.bfloat16)
    pre_act = jnp.dot(normed_share, w_up, preferred_element_type=jnp.float32) + b_up.astype(
        jnp.float32
    )
    hidden_low = gelu_exact(pre_act).astype(jnp.bfloat16)
    ffn_part = jnp.dot(hidden_low, w_down, preferred_element_type=jnp.float32)
    ffn_out = lax.psum(ffn_part, "mp")
    resid_two = normed_one + ffn_out + b_down.astype(jnp.float32)
    out_rows = layer_norm(
        resid_two, gain_two.astype(jnp.float32), shift_two.astype(jnp.float32)
    ).astype(jnp.bfloat16)
    saved_state = (
        proj_low,
        log_total,
        context_low,
        resid_one,
        normed_share,
        pre_act,
        hidden_low,
        resid_two,
    )
    return (out_rows, saved_state)


def backward_pass(tokens_seq, cot_seq, perm_seq, mask_seq, saved_state, weights):
    w_qkv, w_out, gain_one, w_up, w_down, gain_two = weights
    proj_low, log_total, context_low, resid_one, normed_low, pre_act, hidden_low, resid_two = (
        saved_state
    )
    seq_len = tokens_seq.shape[0]
    half_len = seq_len // 2
    local_width = w_qkv.shape[2]
    head_count = local_width // HD
    gain_two_f = gain_two.astype(jnp.float32)
    _, norm_two_back = jax.vjp(layer_norm, resid_two, gain_two_f, jnp.zeros_like(gain_two_f))
    d_resid_two, g_gain_two, g_shift_two = norm_two_back(cot_seq.astype(jnp.float32))
    d_two_share = d_resid_two.astype(jnp.bfloat16)
    g_b_down = jnp.sum(d_resid_two, axis=0)
    g_w_down = contract_rows(hidden_low, d_two_share)
    d_hidden = contract_cols(d_two_share, w_down)
    _, gelu_back = jax.vjp(gelu_exact, pre_act)
    d_pre = gelu_back(d_hidden)[0].astype(jnp.bfloat16)
    g_b_up = jnp.sum(d_pre, axis=0, dtype=jnp.float32)
    g_w_up = contract_rows(normed_low, d_pre)
    d_normed_part = contract_cols(d_pre, w_up)
    d_normed_one = lax.psum(d_normed_part, "mp") + d_resid_two
    gain_one_f = gain_one.astype(jnp.float32)
    _, norm_one_back = jax.vjp(layer_norm, resid_one, gain_one_f, jnp.zeros_like(gain_one_f))
    d_resid_one, g_gain_one, g_shift_one = norm_one_back(d_normed_one)
    d_one_share = d_resid_one.astype(jnp.bfloat16)
    g_b_out = jnp.sum(d_resid_one, axis=0)
    g_w_out = contract_rows(context_low, d_one_share)
    d_context = contract_cols(d_one_share, w_out).astype(jnp.bfloat16)
    query_pair, key_pair, value_pair, swapped = split_pairs(proj_low, perm_seq, head_count)
    allowed, allowed_f, dead_f = pair_pattern(mask_seq, half_len, half_len // 2)
    masked = masked_scores(query_pair, key_pair, allowed)
    attn_prob = jnp.exp(masked - log_total[..., None]) * allowed_f[None]
    d_context_pair = d_context.reshape(2, half_len, head_count, HD)
    d_weights = jnp.einsum(
        "iqhd,ikhd->ihqk", d_context_pair, value_pair, preferred_element_type=jnp.float32
    )
    row_dot = jnp.sum(attn_prob * d_weights, axis=-1, keepdims=True)
    d_scores = (attn_prob * (d_weights - row_dot)).astype(jnp.bfloat16)
    score_scale = HD ** (-0.5)
    d_query = (
        jnp.einsum("ihqk,ikhd->iqhd", d_scores, key_pair, preferred_element_type=jnp.float32)
        * score_scale
    )
    d_key_pair = (
        jnp.einsum("ihqk,iqhd->ikhd", d_scores, query_pair, preferred_element_type=jnp.float32)
        * score_scale
    )
    d_value_pair = jnp.einsum(
        "ihqk,iqhd->ikhd",
        attn_prob.astype(jnp.bfloat16),
        d_context_pair,
        preferred_element_type=jnp.float32,
    )
    d_key = pair_keys(d_key_pair.reshape(seq_len, head_count, HD), swapped)
    d_value = pair_keys(d_value_pair.reshape(seq_len, head_count, HD), swapped)
    d_projected = jnp.stack(
        [
            d_query.reshape(seq_len, local_width),
            d_key.reshape(seq_len, local_width),
            d_value.reshape(seq_len, local_width),
        ],
        axis=1,
    ).astype(jnp.bfloat16)
    g_b_qv = jnp.stack(
        [
            jnp.sum(d_projected[:, 0], axis=0, dtype=jnp.float32),
            jnp.sum(d_projected[:, 2], axis=0, dtype=jnp.float32),
        ]
    )
    g_w_qkv = jnp.einsum("td,tcf->dcf", tokens_seq, d_projected, preferred_element_type=jnp.float32)
    d_input_part = jnp.einsum("tcf,dcf->td", d_projected, w_qkv, preferred_element_type=jnp.float32)
    input_seq = lax.psum(d_input_part.astype(jnp.bfloat16), "mp").astype(jnp.float32) + d_resid_one
    gradients = (
        g_w_qkv,
        g_b_qv,
        g_w_out,
        g_b_out,
        g_gain_one,
        g_shift_one,
        g_w_up,
        g_b_up,
        g_w_down,
        g_b_down,
        g_gain_two,
        g_shift_two,
    )
    return (input_seq, gradients)


def body(
    tokens,
    grad_out,
    head_perm,
    block_mask,
    w_qkv,
    b_qv,
    w_out,
    b_out,
    gain_one,
    shift_one,
    w_up,
    b_up,
    w_down,
    b_down,
    gain_two,
    shift_two,
):
    batch_count = head_perm.shape[0]
    seq_len = tokens.shape[0] // batch_count
    totals = None
    out_parts = []
    input_parts = []
    for batch_index in range(batch_count):
        row_start = batch_index * seq_len
        tokens_seq = tokens[row_start : row_start + seq_len]
        cot_seq = grad_out[row_start : row_start + seq_len]
        perm_seq = head_perm[batch_index]
        mask_seq = block_mask[batch_index]
        forward_weights = (
            lax.all_gather(w_qkv, "dp", axis=0, tiled=True),
            lax.all_gather(b_qv, "dp", axis=1, tiled=True),
            lax.all_gather(w_out, "dp", axis=1, tiled=True),
            lax.all_gather(b_out, "dp", axis=0, tiled=True),
            lax.all_gather(gain_one, "dp", axis=0, tiled=True),
            lax.all_gather(shift_one, "dp", axis=0, tiled=True),
            lax.all_gather(w_up, "dp", axis=0, tiled=True),
            lax.all_gather(b_up, "dp", axis=0, tiled=True),
            lax.all_gather(w_down, "dp", axis=1, tiled=True),
            lax.all_gather(b_down, "dp", axis=0, tiled=True),
            lax.all_gather(gain_two, "dp", axis=0, tiled=True),
            lax.all_gather(shift_two, "dp", axis=0, tiled=True),
        )
        out_seq, saved_state = forward_pass(tokens_seq, perm_seq, mask_seq, forward_weights)
        backward_weights = (
            lax.all_gather(w_qkv, "dp", axis=0, tiled=True),
            lax.all_gather(w_out, "dp", axis=1, tiled=True),
            lax.all_gather(gain_one, "dp", axis=0, tiled=True),
            lax.all_gather(w_up, "dp", axis=0, tiled=True),
            lax.all_gather(w_down, "dp", axis=1, tiled=True),
            lax.all_gather(gain_two, "dp", axis=0, tiled=True),
        )
        input_seq, gradients = backward_pass(
            tokens_seq, cot_seq, perm_seq, mask_seq, saved_state, backward_weights
        )
        if totals is None:
            totals = gradients
        else:
            totals = tuple((summed + latest for summed, latest in zip(totals, gradients)))
        out_parts.append(out_seq)
        input_parts.append(input_seq)
    (
        t_w_qkv,
        t_b_qv,
        t_w_out,
        t_b_out,
        t_gain_one,
        t_shift_one,
        t_w_up,
        t_b_up,
        t_w_down,
        t_b_down,
        t_gain_two,
        t_shift_two,
    ) = totals
    shards = (
        lax.psum_scatter(t_w_qkv, "dp", scatter_dimension=0, tiled=True),
        lax.psum_scatter(t_b_qv, "dp", scatter_dimension=1, tiled=True),
        lax.psum_scatter(t_w_out, "dp", scatter_dimension=1, tiled=True),
        lax.psum_scatter(t_b_out, "dp", scatter_dimension=0, tiled=True),
        lax.psum_scatter(t_gain_one, "dp", scatter_dimension=0, tiled=True),
        lax.psum_scatter(t_shift_one, "dp", scatter_dimension=0, tiled=True),
        lax.psum_scatter(t_w_up, "dp", scatter_dimension=0, tiled=True),
        lax.psum_scatter(t_b_up, "dp", scatter_dimension=0, tiled=True),
        lax.psum_scatter(t_w_down, "dp", scatter_dimension=1, tiled=True),
        lax.psum_scatter(t_b_down, "dp", scatter_dimension=0, tiled=True),
        lax.psum_scatter(t_gain_two, "dp", scatter_dimension=0, tiled=True),
        lax.psum_scatter(t_shift_two, "dp", scatter_dimension=0, tiled=True),
    )
    output = jnp.concatenate(out_parts, axis=0)
    input_grad = jnp.concatenate(input_parts, axis=0)
    return (
        output,
        input_grad,
        shards[0],
        shards[1],
        shards[2],
        shards[3],
        shards[4],
        shards[5],
        shards[6],
        shards[7],
        shards[8],
        shards[9],
        shards[10],
        shards[11],
    )


def solution(mesh):
    placed = (
        P("dp", None),
        P("dp", None),
        P("dp", "mp"),
        P("dp", "mp", None),
        P("dp", None, "mp"),
        P(None, ("mp", "dp")),
        P("mp", "dp"),
        P("dp"),
        P("dp"),
        P("dp"),
        P("dp", "mp"),
        P(("mp", "dp")),
        P("mp", "dp"),
        P("dp"),
        P("dp"),
        P("dp"),
    )
    return jax.shard_map(
        body,
        mesh=mesh,
        in_specs=placed,
        out_specs=(
            P("dp", None),
            P("dp", None),
            P("dp", None, "mp"),
            P(None, ("mp", "dp")),
            P("mp", "dp"),
            P("dp"),
            P("dp"),
            P("dp"),
            P("dp", "mp"),
            P(("mp", "dp")),
            P("mp", "dp"),
            P("dp"),
            P("dp"),
            P("dp"),
        ),
        check_vma=False,
    )
```

profile of v0, /device:TPU:0, one launch (start us, length us, event | category | flops | bytes accessed | tf_op | source)
XLA Modules:
  0.0 1341.1 jit_solution(12367896143275283011)
XLA Ops:
  8.7 23.3 %all-gather = bf16[16,24,2]{1,2,0:T(2,128)(2,1)S(1)} all-gather(bf16[1,24,2]{1,2,0:T(2,128)(2,1)} %bitcast.207), channel_id=1, replica_groups=mesh['dp'=16,'mp'=2] {'dp'}, dimensions={0}, use_global_device_ids=true | all-gather | bytes 1632 | tf_op jit(solution)/shard_map/all_gather | solution.py:253
  32.8 4.4 convert_reduce_fusion.5
  37.3 3.6 convert_element_type.187
  40.9 3.6 convert_element_type.204
  45.8 20.8 %all_gather.26 = bf16[384,768]{0,1:T(8,128)(2,1)} all-gather(bf16[384,48]{0,1:T(8,128)(2,1)S(1)} %copy-done.88), channel_id=1, replica_groups=mesh['dp'=16,'mp'=2] {'dp'}, dimensions={1}, use_global_device_ids=true | all-gather | bytes 626688 | tf_op jit(solution)/shard_map/all_gather | solution.py:254
  66.6 4.0 add_convert_fusion.2
  79.3 3.4 reshape_squeeze.9
  107.5 3.6 concatenate.95
  117.6 4.5 broadcast_select_fusion.2
  130.1 6.4 fusion.56
  149.4 4.3 fusion.53
  165.4 59.2 %all-reduce.20 = (bf16[768]{0:T(1024)(128)(2,1)S(1)}, bf16[768]{0:T(1024)(128)(2,1)S(1)}, bf16[768]{0:T(1024)(128)(2,1)S(1)}, bf16[1536]{0:T(1024)(128)(2,1)S(1)...) all-reduce(bf16[768]{0:T(1024)(128)(2,1)S(1)} %dynamic-update-slice, ...), channel_id=1, replica_groups=mesh['dp'=16,'mp'=2] {'dp'}, use_global_device_ids=true, to_apply=%add | all-reduce | flops 6144 | bytes 24576
  224.6 87.3 %all-reduce.34.cloned.1.call-done = (f32[1024,768]{1,0:T(8,128)}, f32[1024,768]{1,0:T(8,128)}) async-done(((f32[1024,768]{1,0:T(8,128)}, f32[1024,768]{1,0:T(8,128)}), (f32[1024,768]{1,0:T(8,128)}, f32[1024,768]{1,0:T(8,128)})) %all-reduce.34.cloned.1.call-update) | async-done | bytes 6291472 | tf_op jit(solution)/shard_map/psum | solution.py:105
  311.9 4.7 fusion.116
  318.7 37.9 %all-gather.7.cloned.1.call-done = bf16[768,1536]{1,0:T(8,128)(2,1)} async-done(((bf16[48,1536]{1,0:T(8,128)(2,1)}), bf16[768,1536]{1,0:T(8,128)(2,1)}) %all-gather.7.cloned.1.call-update) | async-done | bytes 2359312 | tf_op jit(solution)/shard_map/all_gather | solution.py:258
  356.5 5.5 fusion.101
  364.8 31.7 %multiply_convert_fusion.3 = (bf16[1024,1536]{1,0:T(8,128)(2,1)}, f32[1024,1536]{1,0:T(8,128)}, bf16[1024,1536]{1,0:T(8,128)(2,1)}, f32[1024,1536]{1,0:T(8,128)}, f32[1024,1536]{1,0:T(8,128)}) fusion(f32[1536]{0:T(1024)S(1)} %convert_element_type.196, f32[1024,1536]{1,0:T(8,128)S(1)} %fusion.101, bf16[768,1536]{1,0:T(8,128)(2,1)S(1)} %copy-done.121, ...), kind=kOutput, calls=%fused_computation.34 | convolution fusion | flops 2627469312 | bytes 36982784 | tf_op jit(solution)/shard_map/dot_general | solution.py:109
  399.7 7.1 fusion.129
  406.8 4.3 fusion.131
  411.3 152.0 %all-reduce.32.cloned.1.call-done = (f32[1024,768]{1,0:T(8,128)}, f32[1024,768]{1,0:T(8,128)}) async-done(((f32[1024,768]{1,0:T(8,128)}, f32[1024,768]{1,0:T(8,128)}), (f32[1024,768]{1,0:T(8,128)}, f32[1024,768]{1,0:T(8,128)})) %all-reduce.32.cloned.1.call-update) | async-done | bytes 6291472 | tf_op jit(solution)/shard_map/psum | solution.py:114
  563.3 5.2 fusion.113
  573.8 4.2 fusion.112
  578.0 10.6 convert_reduce_fusion.1
  588.6 4.3 fusion.132
  593.0 7.3 convert_reduce_fusion
  602.0 4.3 fusion.133
  608.3 151.4 %all-reduce.30.cloned.1.call-done = (f32[1024,768]{1,0:T(8,128)}, f32[1024,768]{1,0:T(8,128)}) async-done(((f32[1024,768]{1,0:T(8,128)}, f32[1024,768]{1,0:T(8,128)}), (f32[1024,768]{1,0:T(8,128)}, f32[1024,768]{1,0:T(8,128)})) %all-reduce.30.cloned.1.call-update) | async-done | bytes 6291472 | tf_op jit(solution)/shard_map/psum | solution.py:153
  759.8 5.6 multiply_reduce_fusion.4
  766.3 4.4 multiply_reduce_fusion.5
  777.1 8.8 fusion.44
  797.3 9.8 fusion.41
  809.8 10.2 multiply_reduce_fusion
  820.0 10.3 multiply_convert_fusion
  836.3 10.1 multiply_reduce_fusion.1
  846.4 10.5 multiply_convert_fusion.1
  904.1 3.9 copy.156
  909.4 5.2 bitcast_convert_fusion
  920.1 5.0 fusion.96
  925.1 4.7 convolution_add_fusion
  931.7 5.1 fusion.103
  936.9 4.7 convolution_add_fusion.1
  954.4 70.6 %all-reduce.28.cloned.1.call-done = f32[768,3,384]{2,1,0:T(4,128)} async-done(((f32[768,3,384]{2,1,0:T(4,128)}), f32[768,3,384]{2,1,0:T(4,128)}) %all-reduce.28.cloned.1.call-update) | async-done | bytes 3538960
  1026.8 86.3 %all-reduce.36.cloned.1.call-done = (bf16[1024,768]{1,0:T(8,128)(2,1)}, bf16[1024,768]{1,0:T(8,128)(2,1)}) async-done(((bf16[1024,768]{1,0:T(8,128)(2,1)}, bf16[1024,768]{1,0:T(8,128)(2,1)}), (bf16[1024,768]{1,0:T(8,128)(2,1)}, bf16[1024,768]{1,0:T(8,128)(2,1)})) %all-reduce.36.cloned.1.call-update) | async-done | bytes 3145744 | tf_op jit(solution)/shard_map/psum | solution.py:204
  1113.1 3.7 add_reduce_fusion
  1118.9 62.2 %all-reduce.16 = (f32[2,384]{1,0:T(2,128)S(1)}, f32[768]{0:T(1024)S(1)}, f32[768]{0:T(1024)S(1)}, f32[768]{0:T(1024)S(1)}, f32[1536]{0:T(1024)S(1)}, /*index=5*/...) all-reduce(f32[2,384]{1,0:T(2,128)S(1)} %maximum_add_fusion, ...), channel_id=3, replica_groups=mesh['dp'=16,'mp'=2] {'dp'}, use_global_device_ids=true, to_apply=%region_37.38.clone | all-reduce | flops 6912 | bytes 55296
  1185.8 5.0 pad_maximum_fusion
  1193.5 79.0 %reduce-scatter.7.cloned.1.call-done = f32[48,1536]{1,0:T(8,128)} async-done(((f32[768,1536]{1,0:T(8,128)}), f32[48,1536]{1,0:T(8,128)}) %reduce-scatter.7.cloned.1.call-update) | async-done | bytes 294928 | tf_op jit(solution)/shard_map/reduce_scatter | solution.py:304
  1272.5 61.6 %reduce-scatter.5.cloned.1.call-done = f32[384,48]{0,1:T(8,128)} async-done(((f32[384,768]{0,1:T(8,128)}), f32[384,48]{0,1:T(8,128)}) %reduce-scatter.5.cloned.1.call-update) | async-done | bytes 73744 | tf_op jit(solution)/shard_map/reduce_scatter | solution.py:300
  (495 shorter events, 195.6 us)
Async XLA Ops:
  7.2 59.4 %all-gather.5.cloned.1.call-start = ((), (), s32[]{:S(2)}) async-start(), calls=%async_computation.3 | async-start | bytes 1880064 | tf_op jit(solution)/shard_map/all_gather | solution.py:252
  7.9 304.0 %all-reduce.34.cloned.1.call-start = ((), (), s32[]{:S(2)}) async-start(), calls=%async_computation.12 | async-start | bytes 12582912 | tf_op jit(solution)/shard_map/psum | solution.py:105
  37.3 91.7 %copy-start.2 = (pred[6,512,512]{1,2,0:T(8,128)(4,1)}, pred[6,512,512]{1,2,0:T(8,128)(4,1)S(1)}, u32[]{:S(2)}) copy-start(pred[6,512,512]{1,2,0:T(8,128)(4,1)S(1)} %get-tuple-element.124) | copy-start | bytes 4718596
  37.3 111.0 %copy-start.4 = (pred[6,512,512]{1,2,0:T(8,128)(4,1)}, pred[6,512,512]{1,2,0:T(8,128)(4,1)S(1)}, u32[]{:S(2)}) copy-start(pred[6,512,512]{1,2,0:T(8,128)(4,1)S(1)} %get-tuple-element.155) | copy-start | bytes 4718596
  104.2 13.4 copy-start.117
  128.9 7.5 copy-start.65
  141.4 6.9 copy-start.31
  160.4 196.1 %all-gather.7.cloned.1.call-start = ((), (), s32[]{:S(2)}) async-start(), calls=%async_computation.4 | async-start | bytes 2506752 | tf_op jit(solution)/shard_map/all_gather | solution.py:258
  161.2 238.6 %all-gather.9.cloned.1.call-start = ((), (), s32[]{:S(2)}) async-start(), calls=%async_computation.5 | async-start | bytes 2506752 | tf_op jit(solution)/shard_map/all_gather | solution.py:260
  161.8 401.5 %all-reduce.32.cloned.1.call-start = ((), (), s32[]{:S(2)}) async-start(), calls=%async_computation.11 | async-start | bytes 12582912 | tf_op jit(solution)/shard_map/psum | solution.py:114
  224.6 338.7 %copy-start.108 = (f32[768]{0:T(1024)}, f32[768]{0:T(1024)S(1)}, u32[]{:S(2)}) copy-start(f32[768]{0:T(1024)S(1)} %convert_element_type.194) | copy-start | bytes 9220
  316.6 448.8 %copy-start.7 = (f32[1024,768]{1,0:T(8,128)}, f32[1024,768]{1,0:T(8,128)S(1)}, u32[]{:S(2)}) copy-start(f32[1024,768]{1,0:T(8,128)S(1)} %get-tuple-element.118) | copy-start | bytes 9437188
  318.6 43.5 %copy-start.84 = (f32[1024]{0:T(1024)}, f32[1024]{0:T(1024)S(1)}, u32[]{:S(2)}) copy-start(f32[1024]{0:T(1024)S(1)} %multiply_reduce_fusion.11) | copy-start | bytes 12292
  318.7 446.7 %copy-start.81 = (f32[1024]{0:T(1024)}, f32[1024]{0:T(1024)S(1)}, u32[]{:S(2)}) copy-start(f32[1024]{0:T(1024)S(1)} %fusion.85) | copy-start | bytes 12292
  356.5 8.2 copy-start.121
  399.7 7.1 copy-start.123
  399.7 7.1 copy-start.135
  411.2 348.6 %all-reduce.30.cloned.1.call-start = ((), (), s32[]{:S(2)}) async-start(), calls=%async_computation.10 | async-start | bytes 12582912 | tf_op jit(solution)/shard_map/psum | solution.py:153
  573.7 19.2 %slice-start.8 = ((s8[6291456]{0:T(1024)(128)(4,1)}), s8[4194304]{0:T(1024)(128)(4,1)S(1)}, s32[]{:S(2)}) async-start(s8[6291456]{0:T(1024)(128)(4,1)} %bitcast.208), calls=%async_computation.22 | async-start | bytes 8388608
  578.0 10.6 copy-start.21
  578.0 15.0 %copy-start.24 = (f32[1024,768]{1,0:T(8,128)}, f32[1024,768]{1,0:T(8,128)S(1)}, u32[]{:S(2)}) copy-start(f32[1024,768]{1,0:T(8,128)S(1)} %get-tuple-element.110) | copy-start | bytes 9437188
  578.0 181.8 %copy-start.104 = (f32[1024]{0:T(1024)}, f32[1024]{0:T(1024)S(1)}, u32[]{:S(2)}) copy-start(f32[1024]{0:T(1024)S(1)} %negate_multiply_fusion.3) | copy-start | bytes 12292
  578.0 187.4 %copy-start.106 = (f32[1024]{0:T(1024)}, f32[1024]{0:T(1024)S(1)}, u32[]{:S(2)}) copy-start(f32[1024]{0:T(1024)S(1)} %negate_multiply_fusion.5) | copy-start | bytes 12292
  578.0 10.6 copy-start.122
  578.0 14.9 %slice-start.9 = ((s8[6291456]{0:T(1024)(128)(4,1)}), s8[2097152]{0:T(1024)(128)(4,1)S(1)}, s32[]{:S(2)}) async-start(s8[6291456]{0:T(1024)(128)(4,1)} %bitcast.208), calls=%async_computation.23 | async-start | bytes 4194304
  606.3 418.8 %all-reduce.28.cloned.1.call-start = ((), (), s32[]{:S(2)}) async-start(), calls=%async_computation.9 | async-start | bytes 9437184
  759.8 6.5 copy-start.39
  766.3 6.0 copy-start.37
  777.1 11.4 copy-start.85
  777.1 11.3 copy-start.101
  777.1 11.3 copy-start.15
  793.9 15.9 %slice-start.6 = ((s8[6291456]{0:T(1024)(128)(4,1)}), s8[2097152]{0:T(1024)(128)(4,1)S(1)}, s32[]{:S(2)}) async-start(s8[6291456]{0:T(1024)(128)(4,1)} %bitcast.186), calls=%async_computation.20 | async-start | bytes 4194304
  797.3 12.5 slice-start.7
  820.0 10.3 copy-start.58
  830.3 5.9 slice-start.2
  846.4 10.5 copy-start.56
  861.8 7.6 copy-start.45
  876.5 7.3 copy-start.26
  886.3 8.1 copy-start.27
  890.4 7.9 copy-start.46
  908.1 6.6 copy-start.72
  908.1 6.6 copy-start.76
  908.1 205.0 %all-reduce.36.cloned.1.call-start = ((), (), s32[]{:S(2)}) async-start(), calls=%async_computation.13 | async-start | bytes 6291456 | tf_op jit(solution)/shard_map/psum | solution.py:204
  918.1 7.0 copy-start.105
  918.1 275.4 %reduce-scatter.9.cloned.1.call-start = ((), (), s32[]{:S(2)}) async-start(), calls=%async_computation.8 | async-start | bytes 5013504 | tf_op jit(solution)/shard_map/reduce_scatter | solution.py:306
  929.8 342.7 %reduce-scatter.7.cloned.1.call-start = ((), (), s32[]{:S(2)}) async-start(), calls=%async_computation.7 | async-start | bytes 5013504 | tf_op jit(solution)/shard_map/reduce_scatter | solution.py:304
  941.6 392.5 %reduce-scatter.5.cloned.1.call-start = ((), (), s32[]{:S(2)}) async-start(), calls=%async_computation.6 | async-start | bytes 1253376 | tf_op jit(solution)/shard_map/reduce_scatter | solution.py:300
  1116.8 69.0 %copy-start.19 = (f32[1024,768]{1,0:T(8,128)S(1)}, f32[1024,768]{1,0:T(8,128)}, u32[]{:S(2)}) copy-start(f32[1024,768]{1,0:T(8,128)} %get-tuple-element.135) | copy-start | bytes 9437188
  (113 other events, 368.8 us)
Sparse Core Ops, SparseCore 0:
  10.3 43.1 all-gather.4
  160.6 151.2 all-reduce.33
  314.2 42.3 all-gather.6
  358.7 41.0 all-gather.8
  411.3 151.9 all-reduce.31
  606.5 153.2 all-reduce.29
  908.2 116.8 all-reduce.27
  1027.4 85.5 all-reduce.35
  1117.5 75.9 reduce-scatter.8
  1197.8 74.6 reduce-scatter.6
  1276.7 57.3 reduce-scatter.4
where the time goes:
time: 1350 us; the launch traced here: 1340 us
  waiting for transfers between devices  734 us (54%)
  matrix products  189 us (14%)
  blocking collectives  165 us (12%)
  local copies, waits for them, and re-layouts  128 us (9%)
  other arithmetic  104 us (8%)
  between operations  19.7 us (1%)
    psum x1, waiting for transfers between devices, forward_pass(): ffn_out = lax.psum(ffn_part, 'mp')  152 us
    psum x1, waiting for transfers between devices, backward_pass(): d_normed_one = lax.psum(d_normed_part, 'mp') + d_resid_two  151 us
    unnamed x2, blocking collectives  121 us
    psum x1, waiting for transfers between devices, forward_pass(): attn_out = lax.psum(attn_part, 'mp')  87.3 us
    psum x1, waiting for transfers between devices, backward_pass(): lax.psum(d_input_part.astype(jnp.bfloat16), 'mp').astype(jnp.float32)  86.3 us
    reduce_scatter x1, waiting for transfers between devices, body(): lax.psum_scatter(t_w_up, 'dp', scatter_dimension=0, tiled=True)  79 us
    unnamed x12, waiting for transfers between devices  72.7 us
    reduce_scatter x1, waiting for transfers between devices, body(): lax.psum_scatter(t_w_out, 'dp', scatter_dimension=1, tiled=True)  61.6 us
  transfers between devices with their start and end apart: 11, of which 10 were waited for; matrix products, arithmetic and copies ran while one was open for 9% of the time, Pallas kernels for 0%

commit v1 on v0

--- a/solution.py
+++ b/solution.py
@@ -102,7 +102,7 @@
     )
     context_low = context.reshape(seq_len, local_width).astype(jnp.bfloat16)
     attn_part = jnp.dot(context_low, w_out, preferred_element_type=jnp.float32)
-    attn_out = lax.psum(attn_part, "mp")
+    attn_out = jnp.sum(lax.all_gather(attn_part, "mp"), axis=0)
     resid_one = tokens_seq.astype(jnp.float32) + attn_out + b_out.astype(jnp.float32)
     normed_one = layer_norm(resid_one, gain_one.astype(jnp.float32), shift_one.astype(jnp.float32))
     normed_share = normed_one.astype(jnp.bfloat16)

time: 1350 us -> 1310 us (0.970)
  waiting for transfers between devices: 734 us -> 682 us
    psum x1 -> x0, waiting for transfers between devices: 87.3 us -> none  [forward_pass(): attn_out = lax.psum(attn_part, 'mp')]
    all_gather x0 -> x2, waiting for transfers between devices: none -> 40.4 us  [forward_pass(): attn_out = jnp.sum(lax.all_gather(attn_part, 'mp'), axis=0)]
    unnamed x329 -> x327, local copies, waits for them, and re-layouts: 32.4 us -> 32.2 us
    unnamed x12 -> x13, waiting for transfers between devices: 72.7 us -> 72.5 us
  transfers between devices with their start and end apart: 11 -> 12, of which waited for: 10 -> 10; matrix products, arithmetic and copies ran while one was open for 9% -> 13% of each run, Pallas kernels for 0% -> 0%
where the time goes in v1:
time: 1310 us; the launch traced here: 1300 us
  waiting for transfers between devices  682 us (52%)
  matrix products  189 us (14%)
  blocking collectives  166 us (13%)
  local copies, waits for them, and re-layouts  129 us (10%)
  other arithmetic  116 us (9%)
  between operations  20 us (2%)
    psum x1, waiting for transfers between devices, forward_pass(): ffn_out = lax.psum(ffn_part, 'mp')  152 us
    psum x1, waiting for transfers between devices, backward_pass(): d_normed_one = lax.psum(d_normed_part, 'mp') + d_resid_two  151 us
    unnamed x2, blocking collectives  121 us
    psum x1, waiting for transfers between devices, backward_pass(): lax.psum(d_input_part.astype(jnp.bfloat16), 'mp').astype(jnp.float32)  86.3 us
    reduce_scatter x1, waiting for transfers between devices, body(): lax.psum_scatter(t_w_up, 'dp', scatter_dimension=0, tiled=True)  79.1 us
    unnamed x13, waiting for transfers between devices  72.5 us
    reduce_scatter x1, waiting for transfers between devices, body(): lax.psum_scatter(t_w_out, 'dp', scatter_dimension=1, tiled=True)  61.5 us
    all_gather x2, waiting for transfers between devices, forward_pass(): attn_out = jnp.sum(lax.all_gather(attn_part, 'mp'), axis=0)  40.4 us
  transfers between devices with their start and end apart: 12, of which 10 were waited for; matrix products, arithmetic and copies ran while one was open for 13% of the time, Pallas kernels for 0%

profile of v1, /device:TPU:0, one launch (start us, length us, event | category | flops | bytes accessed | tf_op | source)
XLA Modules:
  0.0 1302.8 jit_solution(2917109372230409095)
XLA Ops:
  8.7 23.3 %all-gather.2 = bf16[16,24,2]{1,2,0:T(2,128)(2,1)S(1)} all-gather(bf16[1,24,2]{1,2,0:T(2,128)(2,1)} %bitcast.211), channel_id=1, replica_groups=mesh['dp'=16,'mp'=2] {'dp'}, dimensions={0}, use_global_device_ids=true | all-gather | bytes 1632 | tf_op jit(solution)/shard_map/all_gather | solution.py:253
  32.8 4.4 convert_reduce_fusion.5
  42.3 21.2 %all_gather.34 = bf16[384,768]{0,1:T(8,128)(2,1)} all-gather(bf16[384,48]{0,1:T(8,128)(2,1)S(1)} %copy-done.85), channel_id=1, replica_groups=mesh['dp'=16,'mp'=2] {'dp'}, dimensions={1}, use_global_device_ids=true | all-gather | bytes 626688 | tf_op jit(solution)/shard_map/all_gather | solution.py:254
  63.5 4.0 add_convert_fusion.3
  89.2 4.5 broadcast_select_fusion.2
  97.1 3.8 multiply_reduce_fusion.3
  101.6 6.2 fusion.56
  113.7 4.1 convert_element_type.204
  153.7 5.1 fusion.53
  169.3 59.1 %all-reduce.19 = (bf16[768]{0:T(1024)(128)(2,1)S(1)}, bf16[768]{0:T(1024)(128)(2,1)S(1)}, bf16[768]{0:T(1024)(128)(2,1)S(1)}, bf16[1536]{0:T(1024)(128)(2,1)S(1)...) all-reduce(bf16[768]{0:T(1024)(128)(2,1)S(1)} %dynamic-update-slice, ...), channel_id=1, replica_groups=mesh['dp'=16,'mp'=2] {'dp'}, use_global_device_ids=true, to_apply=%add | all-reduce | flops 6144 | bytes 24576
  228.4 5.2 reduce_sum.351
  233.7 40.3 %all-gather.17.cloned.1.call-done = f32[2048,768]{1,0:T(8,128)} async-done(((f32[1024,768]{1,0:T(8,128)}), f32[2048,768]{1,0:T(8,128)}) %all-gather.17.cloned.1.call-update) | async-done | bytes 6291472 | tf_op jit(solution)/shard_map/all_gather | solution.py:105
  274.0 5.2 reduce_sum.363
  279.2 4.7 fusion.116
  285.9 32.5 %all-gather.11.cloned.1.call-done = bf16[768,1536]{1,0:T(8,128)(2,1)} async-done(((bf16[48,1536]{1,0:T(8,128)(2,1)}), bf16[768,1536]{1,0:T(8,128)(2,1)}) %all-gather.11.cloned.1.call-update) | async-done | bytes 2359312 | tf_op jit(solution)/shard_map/all_gather | solution.py:258
  318.5 5.5 fusion.101
  326.7 31.6 %multiply_convert_fusion.3 = (bf16[1024,1536]{1,0:T(8,128)(2,1)}, f32[1024,1536]{1,0:T(8,128)}, bf16[1024,1536]{1,0:T(8,128)(2,1)}, f32[1024,1536]{1,0:T(8,128)}, f32[1024,1536]{1,0:T(8,128)}) fusion(f32[1536]{0:T(1024)S(1)} %convert_element_type.196, f32[1024,1536]{1,0:T(8,128)S(1)} %fusion.101, bf16[768,1536]{1,0:T(8,128)(2,1)S(1)} %copy-done.120, ...), kind=kOutput, calls=%fused_computation.34 | convolution fusion | flops 2627469312 | bytes 36982784 | tf_op jit(solution)/shard_map/dot_general | solution.py:109
  361.7 7.1 fusion.129
  368.7 4.3 fusion.131
  373.2 152.0 %all-reduce.30.cloned.1.call-done = (f32[1024,768]{1,0:T(8,128)}, f32[1024,768]{1,0:T(8,128)}) async-done(((f32[1024,768]{1,0:T(8,128)}, f32[1024,768]{1,0:T(8,128)}), (f32[1024,768]{1,0:T(8,128)}, f32[1024,768]{1,0:T(8,128)})) %all-reduce.30.cloned.1.call-update) | async-done | bytes 6291472 | tf_op jit(solution)/shard_map/psum | solution.py:114
  525.2 5.0 fusion.113
  535.4 4.2 fusion.112
  539.7 10.6 convert_reduce_fusion.1
  550.3 4.3 fusion.132
  554.6 7.3 convert_reduce_fusion
  563.6 4.3 fusion.133
  569.8 151.4 %all-reduce.28.cloned.1.call-done = (f32[1024,768]{1,0:T(8,128)}, f32[1024,768]{1,0:T(8,128)}) async-done(((f32[1024,768]{1,0:T(8,128)}, f32[1024,768]{1,0:T(8,128)}), (f32[1024,768]{1,0:T(8,128)}, f32[1024,768]{1,0:T(8,128)})) %all-reduce.28.cloned.1.call-update) | async-done | bytes 6291472 | tf_op jit(solution)/shard_map/psum | solution.py:153
  721.3 5.6 multiply_reduce_fusion.4
  727.8 4.4 multiply_reduce_fusion.5
  738.7 8.8 fusion.44
  758.8 9.8 fusion.41
  771.3 10.2 multiply_reduce_fusion
  781.5 10.3 multiply_convert_fusion
  797.8 10.1 multiply_reduce_fusion.1
  808.0 10.5 multiply_convert_fusion.1
  865.7 3.9 copy.156
  871.0 5.3 bitcast_convert_fusion
  881.6 5.0 fusion.96
  886.7 4.7 convolution_add_fusion
  893.2 5.1 fusion.103
  898.4 4.7 convolution_add_fusion.1
  916.0 70.6 %all-reduce.26.cloned.1.call-done = f32[768,3,384]{2,1,0:T(4,128)} async-done(((f32[768,3,384]{2,1,0:T(4,128)}), f32[768,3,384]{2,1,0:T(4,128)}) %all-reduce.26.cloned.1.call-update) | async-done | bytes 3538960
  988.3 86.3 %all-reduce.32.cloned.1.call-done = (bf16[1024,768]{1,0:T(8,128)(2,1)}, bf16[1024,768]{1,0:T(8,128)(2,1)}) async-done(((bf16[1024,768]{1,0:T(8,128)(2,1)}, bf16[1024,768]{1,0:T(8,128)(2,1)}), (bf16[1024,768]{1,0:T(8,128)(2,1)}, bf16[1024,768]{1,0:T(8,128)(2,1)})) %all-reduce.32.cloned.1.call-update) | async-done | bytes 3145744 | tf_op jit(solution)/shard_map/psum | solution.py:204
  1074.6 3.7 add_reduce_fusion
  1080.4 62.2 %all-reduce.16 = (f32[2,384]{1,0:T(2,128)S(1)}, f32[768]{0:T(1024)S(1)}, f32[768]{0:T(1024)S(1)}, f32[768]{0:T(1024)S(1)}, f32[1536]{0:T(1024)S(1)}, /*index=5*/...) all-reduce(f32[2,384]{1,0:T(2,128)S(1)} %maximum_add_fusion, ...), channel_id=5, replica_groups=mesh['dp'=16,'mp'=2] {'dp'}, use_global_device_ids=true, to_apply=%region_37.38.clone | all-reduce | flops 6912 | bytes 55296
  1147.4 5.0 pad_maximum_fusion
  1154.9 79.1 %reduce-scatter.7.cloned.1.call-done = f32[48,1536]{1,0:T(8,128)} async-done(((f32[768,1536]{1,0:T(8,128)}), f32[48,1536]{1,0:T(8,128)}) %reduce-scatter.7.cloned.1.call-update) | async-done | bytes 294928 | tf_op jit(solution)/shard_map/reduce_scatter | solution.py:304
  1234.0 61.5 %reduce-scatter.5.cloned.1.call-done = f32[384,48]{0,1:T(8,128)} async-done(((f32[384,768]{0,1:T(8,128)}), f32[384,48]{0,1:T(8,128)}) %reduce-scatter.5.cloned.1.call-update) | async-done | bytes 73744 | tf_op jit(solution)/shard_map/reduce_scatter | solution.py:300
  (498 shorter events, 204.6 us)
Async XLA Ops:
  7.2 56.3 %all-gather.9.cloned.1.call-start = ((), (), s32[]{:S(2)}) async-start(), calls=%async_computation.3 | async-start | bytes 1880064 | tf_op jit(solution)/shard_map/all_gather | solution.py:252
  7.9 220.5 %all-gather.15.cloned.1.call-start = ((), (), s32[]{:S(2)}) async-start(), calls=%async_computation.9 | async-start | bytes 9437184 | tf_op jit(solution)/shard_map/all_gather | solution.py:105
  37.2 63.7 %copy-start.2 = (pred[6,512,512]{1,2,0:T(8,128)(4,1)}, pred[6,512,512]{1,2,0:T(8,128)(4,1)S(1)}, u32[]{:S(2)}) copy-start(pred[6,512,512]{1,2,0:T(8,128)(4,1)S(1)} %get-tuple-element.118) | copy-start | bytes 4718596
  37.3 115.6 %copy-start.4 = (pred[6,512,512]{1,2,0:T(8,128)(4,1)}, pred[6,512,512]{1,2,0:T(8,128)(4,1)S(1)}, u32[]{:S(2)}) copy-start(pred[6,512,512]{1,2,0:T(8,128)(4,1)S(1)} %get-tuple-element.153) | copy-start | bytes 4718596
  41.7 25.8 %copy-start.111 = (f32[3,384]{1,0:T(4,128)}, f32[3,384]{1,0:T(4,128)S(1)}, u32[]{:S(2)}) copy-start(f32[3,384]{1,0:T(4,128)S(1)} %maximum_convert_fusion) | copy-start | bytes 13828
  76.1 13.0 %copy-start.116 = (pred[6]{0:T(512)(128)(4,1)S(1)}, pred[6]{0:T(512)(128)(4,1)}, u32[]{:S(2)}) copy-start(pred[6]{0:T(512)(128)(4,1)} %get-tuple-element.182) | copy-start | bytes 22
  100.9 7.0 copy-start.62
  113.6 160.4 %all-gather.17.cloned.1.call-start = ((), (), s32[]{:S(2)}) async-start(), calls=%async_computation.10 | async-start | bytes 9437184 | tf_op jit(solution)/shard_map/all_gather | solution.py:105
  129.1 13.0 copy-start.114
  145.8 7.1 copy-start.31
  161.7 7.1 copy-start.131
  161.7 7.3 copy-start.132
  164.5 153.9 %all-gather.11.cloned.1.call-start = ((), (), s32[]{:S(2)}) async-start(), calls=%async_computation.4 | async-start | bytes 2506752 | tf_op jit(solution)/shard_map/all_gather | solution.py:258
  165.1 196.6 %all-gather.13.cloned.1.call-start = ((), (), s32[]{:S(2)}) async-start(), calls=%async_computation.5 | async-start | bytes 2506752 | tf_op jit(solution)/shard_map/all_gather | solution.py:260
  165.7 359.5 %all-reduce.30.cloned.1.call-start = ((), (), s32[]{:S(2)}) async-start(), calls=%async_computation.13 | async-start | bytes 12582912 | tf_op jit(solution)/shard_map/psum | solution.py:114
  228.4 296.8 %copy-start.105 = (f32[768]{0:T(1024)}, f32[768]{0:T(1024)S(1)}, u32[]{:S(2)}) copy-start(f32[768]{0:T(1024)S(1)} %convert_element_type.194) | copy-start | bytes 9220
  283.8 443.1 %copy-start.7 = (f32[1024,768]{1,0:T(8,128)}, f32[1024,768]{1,0:T(8,128)S(1)}, u32[]{:S(2)}) copy-start(f32[1024,768]{1,0:T(8,128)S(1)} %get-tuple-element.116) | copy-start | bytes 9437188
  285.9 38.1 %copy-start.81 = (f32[1024]{0:T(1024)}, f32[1024]{0:T(1024)S(1)}, u32[]{:S(2)}) copy-start(f32[1024]{0:T(1024)S(1)} %multiply_reduce_fusion.11) | copy-start | bytes 12292
  285.9 441.0 %copy-start.78 = (f32[1024]{0:T(1024)}, f32[1024]{0:T(1024)S(1)}, u32[]{:S(2)}) copy-start(f32[1024]{0:T(1024)S(1)} %fusion.85) | copy-start | bytes 12292
  318.5 8.3 copy-start.120
  361.7 7.1 copy-start.122
  361.7 7.1 copy-start.134
  373.1 348.2 %all-reduce.28.cloned.1.call-start = ((), (), s32[]{:S(2)}) async-start(), calls=%async_computation.12 | async-start | bytes 12582912 | tf_op jit(solution)/shard_map/psum | solution.py:153
  535.4 19.1 %slice-start.8 = ((s8[6291456]{0:T(1024)(128)(4,1)}), s8[4194304]{0:T(1024)(128)(4,1)S(1)}, s32[]{:S(2)}) async-start(s8[6291456]{0:T(1024)(128)(4,1)} %bitcast.212), calls=%async_computation.23 | async-start | bytes 8388608
  539.6 10.6 copy-start.21
  539.6 14.9 %copy-start.24 = (f32[1024,768]{1,0:T(8,128)}, f32[1024,768]{1,0:T(8,128)S(1)}, u32[]{:S(2)}) copy-start(f32[1024,768]{1,0:T(8,128)S(1)} %get-tuple-element.108) | copy-start | bytes 9437188
  539.7 181.6 %copy-start.101 = (f32[1024]{0:T(1024)}, f32[1024]{0:T(1024)S(1)}, u32[]{:S(2)}) copy-start(f32[1024]{0:T(1024)S(1)} %negate_multiply_fusion.3) | copy-start | bytes 12292
  539.7 187.3 %copy-start.103 = (f32[1024]{0:T(1024)}, f32[1024]{0:T(1024)S(1)}, u32[]{:S(2)}) copy-start(f32[1024]{0:T(1024)S(1)} %negate_multiply_fusion.5) | copy-start | bytes 12292
  539.7 10.6 copy-start.121
  539.7 14.9 %slice-start.9 = ((s8[6291456]{0:T(1024)(128)(4,1)}), s8[2097152]{0:T(1024)(128)(4,1)S(1)}, s32[]{:S(2)}) async-start(s8[6291456]{0:T(1024)(128)(4,1)} %bitcast.212), calls=%async_computation.24 | async-start | bytes 4194304
  567.9 418.8 %all-reduce.26.cloned.1.call-start = ((), (), s32[]{:S(2)}) async-start(), calls=%async_computation.11 | async-start | bytes 9437184
  738.6 11.3 copy-start.82
  738.7 11.3 copy-start.98
  738.7 11.3 copy-start.15
  755.4 15.9 %slice-start.6 = ((s8[6291456]{0:T(1024)(128)(4,1)}), s8[2097152]{0:T(1024)(128)(4,1)S(1)}, s32[]{:S(2)}) async-start(s8[6291456]{0:T(1024)(128)(4,1)} %bitcast.188), calls=%async_computation.21 | async-start | bytes 4194304
  758.8 12.5 slice-start.7
  781.5 10.3 copy-start.55
  808.0 10.5 copy-start.53
  823.4 7.6 copy-start.42
  838.0 7.3 copy-start.26
  847.8 8.1 copy-start.27
  851.9 7.9 copy-start.43
  869.6 205.0 %all-reduce.32.cloned.1.call-start = ((), (), s32[]{:S(2)}) async-start(), calls=%async_computation.14 | async-start | bytes 6291456 | tf_op jit(solution)/shard_map/psum | solution.py:204
  879.7 6.9 copy-start.102
  879.7 275.2 %reduce-scatter.9.cloned.1.call-start = ((), (), s32[]{:S(2)}) async-start(), calls=%async_computation.8 | async-start | bytes 5013504 | tf_op jit(solution)/shard_map/reduce_scatter | solution.py:306
  891.4 342.7 %reduce-scatter.7.cloned.1.call-start = ((), (), s32[]{:S(2)}) async-start(), calls=%async_computation.7 | async-start | bytes 5013504 | tf_op jit(solution)/shard_map/reduce_scatter | solution.py:304
  903.2 392.3 %reduce-scatter.5.cloned.1.call-start = ((), (), s32[]{:S(2)}) async-start(), calls=%async_computation.6 | async-start | bytes 1253376 | tf_op jit(solution)/shard_map/reduce_scatter | solution.py:300
  1078.3 69.1 %copy-start.19 = (f32[1024,768]{1,0:T(8,128)S(1)}, f32[1024,768]{1,0:T(8,128)}, u32[]{:S(2)}) copy-start(f32[1024,768]{1,0:T(8,128)} %get-tuple-element.133) | copy-start | bytes 9437188
  (113 other events, 400.6 us)
Sparse Core Ops, SparseCore 0:
  10.3 44.0 all-gather.8
  113.7 78.2 all-gather.14
  193.6 80.3 all-gather.16
  276.1 42.3 all-gather.10
  320.6 41.0 all-gather.12
  373.2 151.9 all-reduce.29
  568.0 153.2 all-reduce.27
  869.7 116.8 all-reduce.25
  989.0 85.5 all-reduce.31
  1078.9 75.9 reduce-scatter.8
  1159.3 74.6 reduce-scatter.6
  1238.1 57.3 reduce-scatter.4
